TPU v7x, 32 devices: a whole 2x2x4 slice. The times are simulated.
32 devices in a mesh: expert: 8 (over z, x), dp: 4 (over y, core).
Axes of the slice: x: 2, y: 2, z: 4, core: 2. Of those that a mesh axis runs over, the one named last changes fastest.
Arguments:
- tokens: bfloat16 [8192, 1024], P(('expert', 'dp')), may hold values from -6 to 6
- route_ids: int32 [8192, 2], P(('expert', 'dp')), may hold values from 0 to 7, all different within a row; in each aligned block of 256 rows (0 to 255, 256 to 511, ...) at most 96 rows name the same one
- gate_values: float32 [8192, 2], P(('expert', 'dp')), may hold values from 0.2 to 1
- w_gate: bfloat16 [8, 1024, 1024], P('expert', 'dp'), may hold values from -0.1875 to 0.1875
- w_up: bfloat16 [8, 1024, 1024], P('expert', 'dp'), may hold values from -0.1875 to 0.1875
- w_down: bfloat16 [8, 1024, 1024], P('expert', 'dp'), may hold values from -0.1875 to 0.1875
- swap_flags: int32 [8], replicated, may hold values from 0 to 1, as said below
- out_grad: bfloat16 [8192, 1024], P(('expert', 'dp')), may hold values from -6 to 6
Outputs:
- layer_out: bfloat16 [8192, 1024], P(('expert', 'dp'))
- grad_tokens: bfloat16 [8192, 1024], P(('expert', 'dp'))
- grad_gate: float32 [8, 1024, 1024], P('expert', 'dp')
- grad_up: float32 [8, 1024, 1024], P('expert', 'dp')
- grad_down: float32 [8, 1024, 1024], P('expert', 'dp')
Inputs may be any that keep to these rules, and one draw needn't show every extreme that they name: `route_ids`: within the rows of one device (256 tokens) no expert is named by more than 96 token-expert pairs, a bound that some block reaches; a token's 2 experts differ. `swap_flags`: the first and the last pair always exchange their experts.
All inputs are finite; a program needn't handle non-finite values.
Results may differ from a plain program's by a relative error of at most 0.012.
Values may be sent and summed in bfloat16 or wider, within the bound.
A program may use at most 64 MiB of HBM per device.

v0:
```python
import functools

import jax
import jax.numpy as jnp
from jax import lax
from jax.experimental import pallas as pl
from jax.experimental.pallas import tpu as pltpu
from jax.sharding import Mesh, PartitionSpec as P

BF = jnp.bfloat16
F32 = jnp.float32
MESH = pl.DeviceIdType.MESH
TILE = 256


def dot(a, b, a_dim, b_dim):
    return lax.dot_general(a, b, (((a_dim,), (b_dim,)), ((), ())), preferred_element_type=F32)


def tile_at(j, size):
    return pl.ds(pl.multiple_of(j * size, size), size)


def kernel(
    nl, nr, cap, flags, tokens, route, gates, out_grad, in_gate, in_up, in_down,
    layer_out, grad_tokens, out_gate, out_up, out_down,
    pick, send_x, send_c, recv_x, recv_c, x_t, h_t, w_gate, w_up, w_down, relay,
    pre_gate, pre_up, hidden, grad_a, grad_b, dw_down, dw_gate, dw_up, from_r, from_y, to_z, from_z,
    send_out, send_grad, ret_out, ret_grad,
    z_s, z_r, y_s, y_r, w_s, w_r, g_s, g_r, d_s, d_r, own_sem,
):
    h, l, b, r = (lax.axis_index(name) for name in ("h", "l", "b", "r"))
    experts = 2 * nl
    rows, n_f = in_gate.shape
    tok = tokens.shape[0]
    slots = experts * cap
    me = b * nl + l
    early = h == b
    late = h != b
    z_dev, y_dev = (1 - h, l, b, r), (h, l, 1 - b, r)
    ins, full = (in_gate, in_up, in_down), (w_gate, w_up, w_down)

    def remote(src, dst, send_sem, recv_sem, dev):
        return pltpu.make_async_remote_copy(
            src_ref=src, dst_ref=dst, send_sem=send_sem, recv_sem=recv_sem,
            device_id=dev, device_id_type=MESH,
        )

    def q_dev(q):
        return (h, lax.rem(q, nl), q // nl, r)

    def r_peer(p):
        return lax.rem(r + p, nr)

    def r_from(p):
        return lax.rem(r + nr - p, nr)

    def shard(side, rest):
        return tile_at(side * nr + rest, rows)

    barrier = pltpu.get_barrier_semaphore()
    peers = [z_dev] + [(h, l, b, r_peer(p)) for p in range(1, nr)]
    peers += [q_dev(lax.rem(me + p, experts)) for p in range(1, experts)]
    for dev in peers:
        pl.semaphore_signal(barrier, inc=1, device_id=dev, device_id_type=MESH)
    pl.semaphore_wait(barrier, len(peers))

    def z_weight(w, dst):
        return remote(ins[w], dst, z_s.at[w], z_r.at[w], z_dev)

    def y_weight(w, src, side):
        return remote(src, full[w].at[shard(side, r)], y_s.at[w], y_r.at[w], y_dev)

    def r_weight(w, group, src, side, p, rest):
        return remote(
            src, full[w].at[shard(side, rest)], w_s.at[w, group, p - 1], w_r.at[w, group, p - 1],
            (h, l, b, r_peer(p)),
        )

    def own_copy(w):
        return pltpu.make_async_copy(ins[w], full[w].at[shard(b, r)], own_sem.at[w])

    def weight_start(w):
        @pl.when(early)
        def _():
            z_weight(w, full[w].at[shard(b, r)]).start()
            own_copy(w).start()
            for p in range(1, nr):
                r_weight(w, 0, ins[w], b, p, r).start()

        @pl.when(late)
        def _():
            z_weight(w, relay.at[w]).start()
            y_weight(w, ins[w], b).start()

    def weight_z(w):
        @pl.when(early)
        def _():
            z_weight(w, relay.at[w]).wait_recv()
            y_weight(w, relay.at[w], b).start()

        @pl.when(late)
        def _():
            z_weight(w, full[w].at[shard(b, r)]).wait_recv()
            for p in range(1, nr):
                r_weight(w, 0, full[w].at[shard(b, r)], b, p, r).start()

    def weight_y(w):
        mine = full[w].at[shard(1 - b, r)]
        y_weight(w, mine, 1 - b).wait_recv()
        for p in range(1, nr):
            r_weight(w, 1, mine, 1 - b, p, r).start()

    def weight_r(w):
        for p in range(1, nr):
            r_weight(w, 0, ins[w], b, p, r_from(p)).wait_recv()
            r_weight(w, 1, ins[w], 1 - b, p, r_from(p)).wait_recv()

        @pl.when(early)
        def _():
            own_copy(w).wait()

    def rows_of(q):
        return tile_at(q, cap)

    def exchange(k, src, dst, p, sender):
        q = lax.rem(me + p, experts)
        return remote(
            src.at[rows_of(q)], dst.at[rows_of(sender)], d_s.at[k, p - 1], d_r.at[k, p - 1], q_dev(q)
        )

    def exchange_start(k, src, dst):
        for p in range(1, experts):
            exchange(k, src, dst, p, me).start()
        dst[rows_of(me), :] = src[rows_of(me), :]

    def exchange_wait(k, src, dst):
        for p in range(1, experts):
            exchange(k, src, dst, p, lax.rem(me + experts - p, experts)).wait_recv()

    parts = (dw_gate, dw_up, dw_down)
    first_flag, second_flag = flags[l], flags[l + nl]
    final_side = jnp.where(first_flag != second_flag, 1 - h, h)
    keep_mine = jnp.where(final_side == b, 1.0, 0.0).astype(F32)

    def r_grad(w, p, side):
        return remote(
            parts[w].at[shard(side, r_peer(p))], from_r.at[w, p - 1, side],
            g_s.at[w, p - 1, side], g_r.at[w, p - 1, side], (h, l, b, r_peer(p)),
        )

    def y_grad(w):
        return remote(parts[w].at[shard(1 - b, r)], from_y.at[w], y_s.at[3 + w], y_r.at[3 + w], y_dev)

    def z_grad(w):
        return remote(to_z.at[w], from_z.at[w], z_s.at[3 + w], z_r.at[3 + w], z_dev)

    def grad_r_start(w):
        for side in range(2):
            for p in range(1, nr):
                r_grad(w, p, side).start()

    chunk = min(rows, 64)

    def grad_sum(w):
        for side in range(2):
            for p in range(1, nr):
                r_grad(w, p, side).wait_recv()

        for side in range(2):
            @pl.loop(0, rows // chunk)
            def _(i):
                at = pl.ds(pl.multiple_of((side * nr + r) * rows + i * chunk, chunk), chunk)
                near = tile_at(i, chunk)
                total = parts[w][at, :].astype(F32)
                for p in range(1, nr):
                    total = total + from_r[w, p - 1, side, near, :].astype(F32)
                parts[w][at, :] = total.astype(BF)
        y_grad(w).start()

    def sides(w, i):
        at = pl.ds(pl.multiple_of((b * nr + r) * rows + i * chunk, chunk), chunk)
        return parts[w][at, :].astype(F32), from_y[w, tile_at(i, chunk), :].astype(F32)

    def grad_z_start(w):
        y_grad(w).wait_recv()

        @pl.loop(0, rows // chunk)
        def _(i):
            mine, other = sides(w, i)
            to_z[w, tile_at(i, chunk), :] = (mine * (1.0 - keep_mine) + other * keep_mine).astype(BF)
        z_grad(w).start()

    def grad_end(w, out):
        z_grad(w).wait_recv()

        @pl.loop(0, rows // chunk)
        def _(i):
            mine, other = sides(w, i)
            kept = mine * keep_mine + other * (1.0 - keep_mine)
            out[tile_at(i, chunk), :] = kept + from_z[w, tile_at(i, chunk), :].astype(F32)

    weight_start(0)

    lanes = lax.broadcasted_iota(jnp.int32, (tok, 128), 1)
    one, two = route[:, 0:1], route[:, 1:2]
    match_one, match_two = one == lanes, two == lanes
    named = (jnp.where(match_one, 1.0, 0.0) + jnp.where(match_two, 1.0, 0.0)).astype(BF)
    row_id = lax.broadcasted_iota(jnp.int32, (tok, tok), 0)
    col_id = lax.broadcasted_iota(jnp.int32, (tok, tok), 1)
    before = dot(jnp.where(col_id < row_id, 1.0, 0.0).astype(BF), named, 1, 0)
    slot_ids = lax.broadcasted_iota(jnp.int32, (tok, slots), 1)
    for k, (ids, match) in enumerate(((one, match_one), (two, match_two))):
        rank = jnp.sum(jnp.where(match, before, 0.0), axis=1, keepdims=True).astype(jnp.int32)
        pick[k] = jnp.where(ids * cap + rank == slot_ids, 1.0, 0.0).astype(BF)
    both = pick[0] + pick[1]

    n_tiles = n_f // TILE
    d_tiles = tokens.shape[1] // TILE
    chosen = both.astype(F32).T.astype(BF)

    @pl.loop(0, d_tiles)
    def _(j):
        send_x[:, tile_at(j, TILE)] = dot(chosen, tokens[:, tile_at(j, TILE)], 1, 0).astype(BF)

    exchange_start(0, send_x, recv_x)
    weight_start(1)
    one_t, two_t = pick[0].astype(F32).T.astype(BF), pick[1].astype(F32).T.astype(BF)

    @pl.loop(0, d_tiles)
    def _(j):
        cot = out_grad[:, tile_at(j, TILE)].astype(F32)
        cot_one = (gates[:, 0:1] * cot).astype(BF)
        cot_two = (gates[:, 1:2] * cot).astype(BF)
        send_c[:, tile_at(j, TILE)] = (dot(one_t, cot_one, 1, 0) + dot(two_t, cot_two, 1, 0)).astype(BF)

    weight_z(0)
    exchange_start(1, send_c, recv_c)
    weight_start(2)
    weight_y(0)
    weight_r(0)
    exchange_wait(0, send_x, recv_x)

    @pl.loop(0, n_tiles)
    def _(j):
        at = tile_at(j, TILE)
        pre_gate[:, at] = dot(recv_x[...], w_gate[:, at], 1, 0)

    @pl.loop(0, d_tiles)
    def _(j):
        at = tile_at(j, TILE)
        x_t[at, :] = recv_x[:, at].T

    weight_z(1)
    weight_y(1)
    weight_r(1)

    @pl.loop(0, n_tiles)
    def _(j):
        at = tile_at(j, TILE)
        up = dot(recv_x[...], w_up[:, at], 1, 0)
        gate = pre_gate[:, at]
        pre_up[:, at] = up
        hid = (gate * jax.nn.sigmoid(gate) * up).astype(BF)
        hidden[:, at] = hid
        h_t[at, :] = hid.T

    exchange_wait(1, send_c, recv_c)

    @pl.loop(0, d_tiles)
    def _(j):
        at = tile_at(j, TILE)
        dw_down[:, at] = dot(h_t[...], recv_c[:, at], 1, 0).astype(BF)

    grad_r_start(2)
    weight_z(2)
    grad_sum(2)
    weight_y(2)
    weight_r(2)

    @pl.loop(0, n_tiles)
    def _(j):
        at = tile_at(j, TILE)
        grad_h = dot(recv_c[...], w_down[at, :], 1, 1)
        gate, up = pre_gate[:, at], pre_up[:, at]
        sig = jax.nn.sigmoid(gate)
        grad_a[:, at] = (grad_h * up * sig * (1.0 + gate * (1.0 - sig))).astype(BF)
        grad_b[:, at] = (grad_h * gate * sig).astype(BF)

    grad_z_start(2)

    @pl.loop(0, n_tiles)
    def _(j):
        at = tile_at(j, TILE)
        dw_gate[:, at] = dot(x_t[...], grad_a[:, at], 1, 0).astype(BF)

    grad_r_start(0)

    @pl.loop(0, n_tiles)
    def _(j):
        at = tile_at(j, TILE)
        dw_up[:, at] = dot(x_t[...], grad_b[:, at], 1, 0).astype(BF)

    grad_r_start(1)
    grad_sum(0)
    grad_sum(1)

    @pl.loop(0, d_tiles)
    def _(j):
        at = tile_at(j, TILE)
        send_out[:, at] = dot(hidden[...], w_down[:, at], 1, 0).astype(BF)

    exchange_start(2, send_out, ret_out)

    @pl.loop(0, d_tiles)
    def _(j):
        at = tile_at(j, TILE)
        send_grad[:, at] = (dot(grad_a[...], w_gate[at, :], 1, 1) + dot(grad_b[...], w_up[at, :], 1, 1)).astype(BF)

    grad_z_start(0)
    exchange_start(3, send_grad, ret_grad)
    grad_z_start(1)
    exchange_wait(2, send_out, ret_out)

    @pl.loop(0, d_tiles)
    def _(j):
        at = tile_at(j, TILE)
        layer_out[:, at] = (
            gates[:, 0:1] * dot(pick[0], ret_out[:, at], 1, 0)
            + gates[:, 1:2] * dot(pick[1], ret_out[:, at], 1, 0)
        ).astype(BF)

    grad_end(2, out_down)
    exchange_wait(3, send_grad, ret_grad)

    @pl.loop(0, d_tiles)
    def _(j):
        at = tile_at(j, TILE)
        grad_tokens[:, at] = dot(pick[0] + pick[1], ret_grad[:, at], 1, 0).astype(BF)

    grad_end(0, out_gate)
    grad_end(1, out_up)

    for w in range(3):
        z_weight(w, relay.at[w]).wait_send()
        y_weight(w, ins[w], b).wait_send()
        z_grad(w).wait_send()
        y_grad(w).wait_send()
        for p in range(1, nr):
            for group in range(2):
                r_weight(w, group, ins[w], b, p, r).wait_send()
                r_grad(w, p, group).wait_send()
    for k, (src, dst) in enumerate(
        ((send_x, recv_x), (send_c, recv_c), (send_out, ret_out), (send_grad, ret_grad))
    ):
        for p in range(1, experts):
            exchange(k, src, dst, p, me).wait_send()


def shards(tokens, route_ids, gate_values, w_gate, w_up, w_down, swap_flags, out_grad):
    nl, nr = lax.axis_size("l"), lax.axis_size("r")
    tok, width = tokens.shape
    rows, n_f = w_gate.shape[1:]
    cap = 3 * tok * route_ids.shape[1] // (4 * nl)
    slots = 2 * nl * cap
    wide = 2 * nr * rows
    vmem = pl.BlockSpec(memory_space=pltpu.VMEM)
    hbm = pl.BlockSpec(memory_space=pl.ANY)
    dma = pltpu.SemaphoreType.DMA
    slot_rows = pltpu.VMEM((slots, width), BF)
    slot_f32 = pltpu.VMEM((slots, n_f), F32)
    weight = pltpu.VMEM((wide, n_f), BF)
    step = pl.pallas_call(
        functools.partial(kernel, nl, nr, cap),
        out_shape=(
            jax.ShapeDtypeStruct((tok, width), BF),
            jax.ShapeDtypeStruct((tok, width), BF),
            jax.ShapeDtypeStruct((rows, n_f), F32),
            jax.ShapeDtypeStruct((rows, n_f), F32),
            jax.ShapeDtypeStruct((rows, n_f), F32),
        ),
        in_specs=[pl.BlockSpec(memory_space=pltpu.SMEM), vmem, vmem, vmem, vmem, hbm, hbm, hbm],
        out_specs=(vmem,) * 5,
        scratch_shapes=[
            pltpu.VMEM((2, tok, slots), BF),
            slot_rows, slot_rows, slot_rows, slot_rows,
            pltpu.VMEM((width, slots), BF), pltpu.VMEM((n_f, slots), BF),
            weight, weight, weight,
            pltpu.VMEM((3, rows, n_f), BF),
            slot_f32, slot_f32,
            slot_rows, slot_rows, slot_rows,
            weight, weight, weight,
            pltpu.VMEM((3, nr - 1, 2, rows, n_f), BF),
            pltpu.VMEM((3, rows, n_f), BF),
            pltpu.VMEM((3, rows, n_f), BF),
            pltpu.VMEM((3, rows, n_f), BF),
            slot_rows, slot_rows, slot_rows, slot_rows,
            dma((6,)), dma((6,)), dma((6,)), dma((6,)),
            dma((3, 2, nr - 1)), dma((3, 2, nr - 1)),
            dma((3, nr - 1, 2)), dma((3, nr - 1, 2)),
            dma((4, 2 * nl - 1)), dma((4, 2 * nl - 1)),
            dma((3,)),
        ],
        compiler_params=pltpu.CompilerParams(
            collective_id=0, has_side_effects=True, vmem_limit_bytes=67043328
        ),
    )
    outs = step(swap_flags, tokens, route_ids, gate_values, out_grad, w_gate[0], w_up[0], w_down[0])
    return outs[0], outs[1], outs[2][None], outs[3][None], outs[4][None]


def solution(mesh):
    n_expert, n_dp = mesh.shape["expert"], mesh.shape["dp"]
    split = Mesh(mesh.devices.reshape(2, n_expert // 2, 2, n_dp // 2), ("h", "l", "b", "r"))
    rows = P(("h", "l", "b", "r"), None)
    weight = P(("h", "l"), ("b", "r"), None)
    return jax.shard_map(
        shards,
        mesh=split,
        in_specs=(rows, rows, rows, weight, weight, weight, P(), rows),
        out_specs=(rows, rows, weight, weight, weight),
        check_vma=False,
    )
```

profile of v0, /device:TPU:0, one launch (start us, length us, event | category | flops | bytes accessed | tf_op | source)
XLA Modules:
  0.0 203.3 jit_solution(15107529903101079977)
XLA Ops:
  0.6 0.0 copy-start.4
  0.6 0.7 copy-done.4
  1.3 0.0 copy-start.5
  1.3 0.8 copy.13.route
  2.1 0.0 copy-done.5
  2.1 0.8 copy.14.gates
  2.9 193.4 %shard_map.119 = (bf16[256,1024]{1,0:T(8,128)(2,1)}, bf16[256,1024]{1,0:T(8,128)(2,1)}, f32[256,1024]{1,0:T(8,128)}, f32[256,1024]{1,0:T(8,128)}, f32[256,1024]{1,0:T(8,128)}) custom-call(s32[8]{0:T(128)} %flags.1, bf16[256,1024]{1,0:T(8,128)(2,1)} %tokens.1, s32[256,2]{1,0:T(8,128)} %copy.13.route, f32[256,2]{1,0:T(8,128)} %copy.14.gates, ...), custom_call_target="tpu_custom_call" | custom-call | tf_op jit(solution)/shard_map/pallas_call | solution.py:408
  196.3 0.0 copy-start.3
  196.3 0.0 copy-start.2
  196.4 2.0 copy.20
  198.3 0.0 copy-done.3
  198.3 0.8 copy.21
  199.1 0.0 copy-done.2
  199.1 0.0 copy-start.1
  199.1 1.0 copy.22
  200.1 0.6 copy-done.1
  200.7 0.0 copy-start
  200.7 1.0 copy.23
  201.7 0.6 copy-done
  202.3 1.0 copy.24
Async XLA Ops:
  0.6 0.7 copy-start.4
  1.3 0.8 copy-start.5
  196.3 2.0 copy-start.3
  196.3 2.8 %copy-start.2 = (f32[256,1024]{1,0:T(8,128)S(1)}, f32[256,1024]{1,0:T(8,128)}, u32[]{:S(2)}) copy-start(f32[256,1024]{1,0:T(8,128)} %get-tuple-element.12) | copy-start | bytes 3145732
  199.1 1.6 copy-start.1
  200.7 1.6 copy-start
where the time goes:
time: 206 us; the launch traced here: 203 us
  Pallas kernels  193 us (94%)
  local copies, waits for them, and re-layouts  9.24 us (4%)
    pallas_call x1, Pallas kernels, shards(): step(swap_flags, tokens, route_ids, gate_values, out_grad, w_gate[0], w_u...  193 us
    unnamed x19, local copies, waits for them, and re-layouts  9.24 us

commit v1 on v0

--- a/solution.py
+++ b/solution.py
@@ -22,11 +22,11 @@
 
 
 def kernel(
-    nl, nr, cap, flags, tokens, route, gates, out_grad, in_gate, in_up, in_down,
+    nl, nr, cap, flags, tokens, route_t, gates_t, out_grad, in_gate, in_up, in_down,
     layer_out, grad_tokens, out_gate, out_up, out_down,
     pick, send_x, send_c, recv_x, recv_c, x_t, h_t, w_gate, w_up, w_down, relay,
     pre_gate, pre_up, hidden, grad_a, grad_b, dw_down, dw_gate, dw_up, from_r, from_y, to_z, from_z,
-    send_out, send_grad, ret_out, ret_grad,
+    send_out, send_grad, ret_out, ret_grad, gates,
     z_s, z_r, y_s, y_r, w_s, w_r, g_s, g_r, d_s, d_r, own_sem,
 ):
     h, l, b, r = (lax.axis_index(name) for name in ("h", "l", "b", "r"))
@@ -124,19 +124,21 @@
         return tile_at(q, cap)
 
     def exchange(k, src, dst, p, sender):
-        q = lax.rem(me + p, experts)
+        q = lax.rem(b + p // nl, 2) * nl + lax.rem(l + p % nl, nl)
         return remote(
             src.at[rows_of(q)], dst.at[rows_of(sender)], d_s.at[k, p - 1], d_r.at[k, p - 1], q_dev(q)
         )
 
-    def exchange_start(k, src, dst):
-        for p in range(1, experts):
+    def exchange_start(k, src, dst, across):
+        for p in range(nl, experts) if across else range(1, nl):
             exchange(k, src, dst, p, me).start()
-        dst[rows_of(me), :] = src[rows_of(me), :]
+        if not across:
+            dst[rows_of(me), :] = src[rows_of(me), :]
 
     def exchange_wait(k, src, dst):
         for p in range(1, experts):
-            exchange(k, src, dst, p, lax.rem(me + experts - p, experts)).wait_recv()
+            sender = lax.rem(b + p // nl, 2) * nl + lax.rem(l + nl - p % nl, nl)
+            exchange(k, src, dst, p, sender).wait_recv()
 
     parts = (dw_gate, dw_up, dw_down)
     first_flag, second_flag = flags[l], flags[l + nl]
@@ -176,7 +178,6 @@
                 for p in range(1, nr):
                     total = total + from_r[w, p - 1, side, near, :].astype(F32)
                 parts[w][at, :] = total.astype(BF)
-        y_grad(w).start()
 
     def sides(w, i):
         at = pl.ds(pl.multiple_of((b * nr + r) * rows + i * chunk, chunk), chunk)
@@ -202,12 +203,18 @@
 
     weight_start(0)
 
+    row_id = lax.broadcasted_iota(jnp.int32, (tok, tok), 0)
+    col_id = lax.broadcasted_iota(jnp.int32, (tok, tok), 1)
+
+    def column(line):
+        return jnp.sum(jnp.where(row_id == col_id, line, 0.0), axis=1, keepdims=True)
+
+    for k in range(2):
+        gates[:, k : k + 1] = column(gates_t[k : k + 1, :])
+    one, two = (column(route_t[k : k + 1, :].astype(F32)).astype(jnp.int32) for k in range(2))
     lanes = lax.broadcasted_iota(jnp.int32, (tok, 128), 1)
-    one, two = route[:, 0:1], route[:, 1:2]
     match_one, match_two = one == lanes, two == lanes
     named = (jnp.where(match_one, 1.0, 0.0) + jnp.where(match_two, 1.0, 0.0)).astype(BF)
-    row_id = lax.broadcasted_iota(jnp.int32, (tok, tok), 0)
-    col_id = lax.broadcasted_iota(jnp.int32, (tok, tok), 1)
     before = dot(jnp.where(col_id < row_id, 1.0, 0.0).astype(BF), named, 1, 0)
     slot_ids = lax.broadcasted_iota(jnp.int32, (tok, slots), 1)
     for k, (ids, match) in enumerate(((one, match_one), (two, match_two))):
@@ -223,7 +230,8 @@
     def _(j):
         send_x[:, tile_at(j, TILE)] = dot(chosen, tokens[:, tile_at(j, TILE)], 1, 0).astype(BF)
 
-    exchange_start(0, send_x, recv_x)
+    exchange_start(0, send_x, recv_x, False)
+    exchange_start(0, send_x, recv_x, True)
     weight_start(1)
     one_t, two_t = pick[0].astype(F32).T.astype(BF), pick[1].astype(F32).T.astype(BF)
 
@@ -235,7 +243,8 @@
         send_c[:, tile_at(j, TILE)] = (dot(one_t, cot_one, 1, 0) + dot(two_t, cot_two, 1, 0)).astype(BF)
 
     weight_z(0)
-    exchange_start(1, send_c, recv_c)
+    exchange_start(1, send_c, recv_c, False)
+    exchange_start(1, send_c, recv_c, True)
     weight_start(2)
     weight_y(0)
     weight_r(0)
@@ -275,6 +284,7 @@
     grad_r_start(2)
     weight_z(2)
     grad_sum(2)
+    y_grad(2).start()
     weight_y(2)
     weight_r(2)
 
@@ -287,38 +297,44 @@
         grad_a[:, at] = (grad_h * up * sig * (1.0 + gate * (1.0 - sig))).astype(BF)
         grad_b[:, at] = (grad_h * gate * sig).astype(BF)
 
+    @pl.loop(0, d_tiles)
+    def _(j):
+        at = tile_at(j, TILE)
+        send_out[:, at] = dot(hidden[...], w_down[:, at], 1, 0).astype(BF)
+
+    exchange_start(2, send_out, ret_out, False)
+
+    @pl.loop(0, n_tiles)
+    def _(j):
+        at = tile_at(j, TILE)
+        dw_gate[:, at] = dot(x_t[...], grad_a[:, at], 1, 0).astype(BF)
+
+    grad_r_start(0)
     grad_z_start(2)
+    grad_sum(0)
+    y_grad(0).start()
 
     @pl.loop(0, n_tiles)
     def _(j):
         at = tile_at(j, TILE)
-        dw_gate[:, at] = dot(x_t[...], grad_a[:, at], 1, 0).astype(BF)
-
-    grad_r_start(0)
-
-    @pl.loop(0, n_tiles)
-    def _(j):
-        at = tile_at(j, TILE)
         dw_up[:, at] = dot(x_t[...], grad_b[:, at], 1, 0).astype(BF)
 
     grad_r_start(1)
-    grad_sum(0)
+
+    @pl.loop(0, d_tiles)
+    def _(j):
+        at = tile_at(j, TILE)
+        send_grad[:, at] = (dot(grad_a[...], w_gate[at, :], 1, 1) + dot(grad_b[...], w_up[at, :], 1, 1)).astype(BF)
+
+    exchange_start(3, send_grad, ret_grad, False)
     grad_sum(1)
-
-    @pl.loop(0, d_tiles)
-    def _(j):
-        at = tile_at(j, TILE)
-        send_out[:, at] = dot(hidden[...], w_down[:, at], 1, 0).astype(BF)
-
-    exchange_start(2, send_out, ret_out)
-
-    @pl.loop(0, d_tiles)
-    def _(j):
-        at = tile_at(j, TILE)
-        send_grad[:, at] = (dot(grad_a[...], w_gate[at, :], 1, 1) + dot(grad_b[...], w_up[at, :], 1, 1)).astype(BF)
-
+    y_grad(0).wait_send()
+    y_grad(1).start()
     grad_z_start(0)
-    exchange_start(3, send_grad, ret_grad)
+
+    y_grad(1).wait_send()
+    exchange_start(2, send_out, ret_out, True)
+    exchange_start(3, send_grad, ret_grad, True)
     grad_z_start(1)
     exchange_wait(2, send_out, ret_out)
 
@@ -341,11 +357,11 @@
     grad_end(0, out_gate)
     grad_end(1, out_up)
 
+    y_grad(2).wait_send()
     for w in range(3):
         z_weight(w, relay.at[w]).wait_send()
         y_weight(w, ins[w], b).wait_send()
         z_grad(w).wait_send()
-        y_grad(w).wait_send()
         for p in range(1, nr):
             for group in range(2):
                 r_weight(w, group, ins[w], b, p, r).wait_send()
@@ -355,6 +371,15 @@
     ):
         for p in range(1, experts):
             exchange(k, src, dst, p, me).wait_send()
+
+
+def store(*refs):
+    sems = refs[-1]
+    copies = [pltpu.make_async_copy(refs[i], refs[5 + i], sems.at[i]) for i in range(5)]
+    for copy in copies:
+        copy.start()
+    for copy in copies:
+        copy.wait()
 
 
 def shards(tokens, route_ids, gate_values, w_gate, w_up, w_down, swap_flags, out_grad):
@@ -395,6 +420,7 @@
             pltpu.VMEM((3, rows, n_f), BF),
             pltpu.VMEM((3, rows, n_f), BF),
             slot_rows, slot_rows, slot_rows, slot_rows,
+            pltpu.VMEM((tok, 2), F32),
             dma((6,)), dma((6,)), dma((6,)), dma((6,)),
             dma((3, 2, nr - 1)), dma((3, 2, nr - 1)),
             dma((3, nr - 1, 2)), dma((3, nr - 1, 2)),
@@ -405,7 +431,14 @@
             collective_id=0, has_side_effects=True, vmem_limit_bytes=67043328
         ),
     )
-    outs = step(swap_flags, tokens, route_ids, gate_values, out_grad, w_gate[0], w_up[0], w_down[0])
+    outs = step(swap_flags, tokens, route_ids.T, gate_values.T, out_grad, w_gate[0], w_up[0], w_down[0])
+    outs = pl.pallas_call(
+        store,
+        out_shape=tuple(jax.ShapeDtypeStruct(out.shape, out.dtype) for out in outs),
+        in_specs=[vmem] * 5,
+        out_specs=(hbm,) * 5,
+        scratch_shapes=[dma((5,))],
+    )(*outs)
     return outs[0], outs[1], outs[2][None], outs[3][None], outs[4][None]
 
 

time: 206 us -> 183 us (0.89)
  the two profiles are of different devices: /device:TPU:0 before, /device:TPU:6 now
where the time goes in v1:
time: 183 us
  Pallas kernels  182 us (99%)
    pallas_call x1, Pallas kernels, shards(): step(swap_flags, tokens, route_ids.T, gate_values.T, out_grad, w_gate[0],...  178 us
    pallas_call x1, Pallas kernels, shards(): pl.pallas_call(store, out_shape=tuple((jax.ShapeDtypeStruct(out.shape, ou...  4.23 us

profile of v1, /device:TPU:6, one launch (start us, length us, event | category | flops | bytes accessed | tf_op | source)
XLA Modules:
  0.0 182.6 jit_solution(5276205137471329349)
XLA Ops:
  0.6 177.7 %shard_map.119 = (bf16[256,1024]{1,0:T(8,128)(2,1)}, bf16[256,1024]{1,0:T(8,128)(2,1)}, f32[256,1024]{1,0:T(8,128)}, f32[256,1024]{1,0:T(8,128)}, f32[256,1024]{1,0:T(8,128)}) custom-call(s32[8]{0:T(128)} %flags.1, bf16[256,1024]{1,0:T(8,128)(2,1)} %tokens.1, s32[2,256]{1,0:T(2,128)} %bitcast.11, f32[2,256]{1,0:T(2,128)} %bitcast.12, ...), custom_call_target="tpu_custom_call" | custom-call | tf_op jit(solution)/shard_map/pallas_call | solution.py:434
  178.4 4.2 %shard_map.120 = (bf16[256,1024]{1,0:T(8,128)(2,1)}, bf16[256,1024]{1,0:T(8,128)(2,1)}, f32[256,1024]{1,0:T(8,128)}, f32[256,1024]{1,0:T(8,128)}, f32[256,1024]{1,0:T(8,128)}) custom-call(bf16[256,1024]{1,0:T(8,128)(2,1)} %get-tuple-element.15.refs_0_, bf16[256,1024]{1,0:T(8,128)(2,1)} %get-tuple-element.16.refs_1_, f32[256,1024]{1,0:T(8,128)} %get-tuple-element.17.refs_2_, ...), custom_call_target="tpu_custom_call" | custom-call | tf_op jit(solution)/shard_map/pallas_call | solution.py:435

commit v2 on v1

--- a/solution.py
+++ b/solution.py
@@ -11,6 +11,7 @@
 F32 = jnp.float32
 MESH = pl.DeviceIdType.MESH
 TILE = 256
+PIECES = 2
 
 
 def dot(a, b, a_dim, b_dim):
@@ -26,8 +27,8 @@
     layer_out, grad_tokens, out_gate, out_up, out_down,
     pick, send_x, send_c, recv_x, recv_c, x_t, h_t, w_gate, w_up, w_down, relay,
     pre_gate, pre_up, hidden, grad_a, grad_b, dw_down, dw_gate, dw_up, from_r, from_y, to_z, from_z,
-    send_out, send_grad, ret_out, ret_grad, gates,
-    z_s, z_r, y_s, y_r, w_s, w_r, g_s, g_r, d_s, d_r, own_sem,
+    send_out, send_grad, ret_out, ret_grad, gates, gates_far, near, far, route_p, gates_p, far_send, far_recv,
+    z_s, z_r, y_s, y_r, w_s, w_r, g_s, g_r, d_s, d_r, own_sem, p_s, p_r, f_s, f_r,
 ):
     h, l, b, r = (lax.axis_index(name) for name in ("h", "l", "b", "r"))
     experts = 2 * nl
@@ -65,16 +66,24 @@
         pl.semaphore_signal(barrier, inc=1, device_id=dev, device_id_type=MESH)
     pl.semaphore_wait(barrier, len(peers))
 
-    def z_weight(w, dst):
-        return remote(ins[w], dst, z_s.at[w], z_r.at[w], z_dev)
-
-    def y_weight(w, src, side):
-        return remote(src, full[w].at[shard(side, r)], y_s.at[w], y_r.at[w], y_dev)
-
-    def r_weight(w, group, src, side, p, rest):
+    piece_rows = rows // PIECES
+
+    def piece(i):
+        return pl.ds(i * piece_rows, piece_rows)
+
+    def shard_piece(side, rest, i):
+        return pl.ds(pl.multiple_of((side * nr + rest) * rows + i * piece_rows, piece_rows), piece_rows)
+
+    def z_weight(w, i, dst):
+        return remote(ins[w].at[piece(i)], dst, z_s.at[w, i], z_r.at[w, i], z_dev)
+
+    def y_weight(w, i, src, side):
+        return remote(src, full[w].at[shard_piece(side, r, i)], y_s.at[w, i], y_r.at[w, i], y_dev)
+
+    def r_weight(w, i, group, src, side, p, rest):
         return remote(
-            src, full[w].at[shard(side, rest)], w_s.at[w, group, p - 1], w_r.at[w, group, p - 1],
-            (h, l, b, r_peer(p)),
+            src, full[w].at[shard_piece(side, rest, i)],
+            w_s.at[w, i, group, p - 1], w_r.at[w, i, group, p - 1], (h, l, b, r_peer(p)),
         )
 
     def own_copy(w):
@@ -83,38 +92,44 @@
     def weight_start(w):
         @pl.when(early)
         def _():
-            z_weight(w, full[w].at[shard(b, r)]).start()
+            for i in range(PIECES):
+                z_weight(w, i, full[w].at[shard_piece(b, r, i)]).start()
             own_copy(w).start()
-            for p in range(1, nr):
-                r_weight(w, 0, ins[w], b, p, r).start()
+            for i in range(PIECES):
+                for p in range(1, nr):
+                    r_weight(w, i, 0, ins[w].at[piece(i)], b, p, r).start()
 
         @pl.when(late)
         def _():
-            z_weight(w, relay.at[w]).start()
-            y_weight(w, ins[w], b).start()
-
-    def weight_z(w):
+            for i in range(PIECES):
+                z_weight(w, i, relay.at[w, piece(i)]).start()
+                y_weight(w, i, ins[w].at[piece(i)], b).start()
+
+    def weight_z(w, i):
         @pl.when(early)
         def _():
-            z_weight(w, relay.at[w]).wait_recv()
-            y_weight(w, relay.at[w], b).start()
+            z_weight(w, i, relay.at[w, piece(i)]).wait_recv()
+            y_weight(w, i, relay.at[w, piece(i)], b).start()
 
         @pl.when(late)
         def _():
-            z_weight(w, full[w].at[shard(b, r)]).wait_recv()
+            mine = full[w].at[shard_piece(b, r, i)]
+            z_weight(w, i, mine).wait_recv()
             for p in range(1, nr):
-                r_weight(w, 0, full[w].at[shard(b, r)], b, p, r).start()
+                r_weight(w, i, 0, mine, b, p, r).start()
 
     def weight_y(w):
-        mine = full[w].at[shard(1 - b, r)]
-        y_weight(w, mine, 1 - b).wait_recv()
-        for p in range(1, nr):
-            r_weight(w, 1, mine, 1 - b, p, r).start()
+        for i in range(PIECES):
+            mine = full[w].at[shard_piece(1 - b, r, i)]
+            y_weight(w, i, mine, 1 - b).wait_recv()
+            for p in range(1, nr):
+                r_weight(w, i, 1, mine, 1 - b, p, r).start()
 
     def weight_r(w):
-        for p in range(1, nr):
-            r_weight(w, 0, ins[w], b, p, r_from(p)).wait_recv()
-            r_weight(w, 1, ins[w], 1 - b, p, r_from(p)).wait_recv()
+        for i in range(PIECES):
+            for p in range(1, nr):
+                r_weight(w, i, 0, ins[w].at[piece(i)], b, p, r_from(p)).wait_recv()
+                r_weight(w, i, 1, ins[w].at[piece(i)], 1 - b, p, r_from(p)).wait_recv()
 
         @pl.when(early)
         def _():
@@ -140,6 +155,28 @@
             sender = lax.rem(b + p // nl, 2) * nl + lax.rem(l + nl - p % nl, nl)
             exchange(k, src, dst, p, sender).wait_recv()
 
+    def back(k, src, dst, t, dl, sender):
+        at = lax.rem(l + dl, nl)
+        return remote(
+            src.at[rows_of(lax.rem(b + t, 2) * nl + at)], dst.at[rows_of(t * nl + sender)],
+            d_s.at[k, t * nl + dl - 1], d_r.at[k, t * nl + dl - 1], (h, at, b, r),
+        )
+
+    def back_start(k, src, dst, t):
+        for dl in range(1, nl):
+            back(k, src, dst, t, dl, l).start()
+        dst[rows_of(t * nl + l), :] = src[rows_of(lax.rem(b + t, 2) * nl + l), :]
+
+    def back_wait(k, src, dst, t):
+        for dl in range(1, nl):
+            back(k, src, dst, t, dl, lax.rem(l + nl - dl, nl)).wait_recv()
+
+    def info(i):
+        return remote((route_t, gates_t)[i], (route_p, gates_p)[i], p_s.at[i], p_r.at[i], y_dev)
+
+    def far_copy(i):
+        return remote(far_send.at[i], far_recv.at[i], f_s.at[i], f_r.at[i], y_dev)
+
     parts = (dw_gate, dw_up, dw_down)
     first_flag, second_flag = flags[l], flags[l + nl]
     final_side = jnp.where(first_flag != second_flag, 1 - h, h)
@@ -151,18 +188,31 @@
             g_s.at[w, p - 1, side], g_r.at[w, p - 1, side], (h, l, b, r_peer(p)),
         )
 
-    def y_grad(w):
-        return remote(parts[w].at[shard(1 - b, r)], from_y.at[w], y_s.at[3 + w], y_r.at[3 + w], y_dev)
-
-    def z_grad(w):
-        return remote(to_z.at[w], from_z.at[w], z_s.at[3 + w], z_r.at[3 + w], z_dev)
+    def y_grad(w, i):
+        return remote(
+            parts[w].at[shard_piece(1 - b, r, i)], from_y.at[w, piece(i)],
+            y_s.at[3 + w, i], y_r.at[3 + w, i], y_dev,
+        )
+
+    def y_grad_start(w):
+        for i in range(PIECES):
+            y_grad(w, i).start()
+
+    def y_grad_sent(w):
+        for i in range(PIECES):
+            y_grad(w, i).wait_send()
+
+    def z_grad(w, i):
+        return remote(
+            to_z.at[w, piece(i)], from_z.at[w, piece(i)], z_s.at[3 + w, i], z_r.at[3 + w, i], z_dev
+        )
 
     def grad_r_start(w):
         for side in range(2):
             for p in range(1, nr):
                 r_grad(w, p, side).start()
 
-    chunk = min(rows, 64)
+    chunk = min(piece_rows, 64)
 
     def grad_sum(w):
         for side in range(2):
@@ -184,16 +234,18 @@
         return parts[w][at, :].astype(F32), from_y[w, tile_at(i, chunk), :].astype(F32)
 
     def grad_z_start(w):
-        y_grad(w).wait_recv()
-
-        @pl.loop(0, rows // chunk)
-        def _(i):
-            mine, other = sides(w, i)
-            to_z[w, tile_at(i, chunk), :] = (mine * (1.0 - keep_mine) + other * keep_mine).astype(BF)
-        z_grad(w).start()
+        for k in range(PIECES):
+            y_grad(w, k).wait_recv()
+
+            @pl.loop(k * piece_rows // chunk, (k + 1) * piece_rows // chunk)
+            def _(i):
+                mine, other = sides(w, i)
+                to_z[w, tile_at(i, chunk), :] = (mine * (1.0 - keep_mine) + other * keep_mine).astype(BF)
+            z_grad(w, k).start()
 
     def grad_end(w, out):
-        z_grad(w).wait_recv()
+        for k in range(PIECES):
+            z_grad(w, k).wait_recv()
 
         @pl.loop(0, rows // chunk)
         def _(i):
@@ -203,23 +255,34 @@
 
     weight_start(0)
 
+    info(0).start()
+    info(1).start()
     row_id = lax.broadcasted_iota(jnp.int32, (tok, tok), 0)
     col_id = lax.broadcasted_iota(jnp.int32, (tok, tok), 1)
 
     def column(line):
         return jnp.sum(jnp.where(row_id == col_id, line, 0.0), axis=1, keepdims=True)
 
+    def slots_of(lines):
+        one, two = (column(lines[k : k + 1, :].astype(F32)).astype(jnp.int32) for k in range(2))
+        lanes = lax.broadcasted_iota(jnp.int32, (tok, 128), 1)
+        match_one, match_two = one == lanes, two == lanes
+        named = (jnp.where(match_one, 1.0, 0.0) + jnp.where(match_two, 1.0, 0.0)).astype(BF)
+        before = dot(jnp.where(col_id < row_id, 1.0, 0.0).astype(BF), named, 1, 0)
+        places = []
+        for ids, match in ((one, match_one), (two, match_two)):
+            rank = jnp.sum(jnp.where(match, before, 0.0), axis=1, keepdims=True).astype(jnp.int32)
+            places.append(ids * cap + rank)
+        return places
+
     for k in range(2):
         gates[:, k : k + 1] = column(gates_t[k : k + 1, :])
-    one, two = (column(route_t[k : k + 1, :].astype(F32)).astype(jnp.int32) for k in range(2))
-    lanes = lax.broadcasted_iota(jnp.int32, (tok, 128), 1)
-    match_one, match_two = one == lanes, two == lanes
-    named = (jnp.where(match_one, 1.0, 0.0) + jnp.where(match_two, 1.0, 0.0)).astype(BF)
-    before = dot(jnp.where(col_id < row_id, 1.0, 0.0).astype(BF), named, 1, 0)
     slot_ids = lax.broadcasted_iota(jnp.int32, (tok, slots), 1)
-    for k, (ids, match) in enumerate(((one, match_one), (two, match_two))):
-        rank = jnp.sum(jnp.where(match, before, 0.0), axis=1, keepdims=True).astype(jnp.int32)
-        pick[k] = jnp.where(ids * cap + rank == slot_ids, 1.0, 0.0).astype(BF)
+    half = nl * cap
+    side_ids = lax.broadcasted_iota(jnp.int32, (tok, half), 1) + b * half
+    for k, place in enumerate(slots_of(route_t)):
+        pick[k] = jnp.where(place == slot_ids, 1.0, 0.0).astype(BF)
+        near[k] = jnp.where(place == side_ids, 1.0, 0.0).astype(BF)
     both = pick[0] + pick[1]
 
     n_tiles = n_f // TILE
@@ -242,8 +305,9 @@
         cot_two = (gates[:, 1:2] * cot).astype(BF)
         send_c[:, tile_at(j, TILE)] = (dot(one_t, cot_one, 1, 0) + dot(two_t, cot_two, 1, 0)).astype(BF)
 
-    weight_z(0)
     exchange_start(1, send_c, recv_c, False)
+    weight_z(0, 0)
+    weight_z(0, 1)
     exchange_start(1, send_c, recv_c, True)
     weight_start(2)
     weight_y(0)
@@ -260,7 +324,15 @@
         at = tile_at(j, TILE)
         x_t[at, :] = recv_x[:, at].T
 
-    weight_z(1)
+    info(0).wait_recv()
+    info(1).wait_recv()
+    for k in range(2):
+        gates_far[:, k : k + 1] = column(gates_p[k : k + 1, :])
+    for k, place in enumerate(slots_of(route_p)):
+        far[k] = jnp.where(place == side_ids, 1.0, 0.0).astype(BF)
+
+    weight_z(1, 0)
+    weight_z(1, 1)
     weight_y(1)
     weight_r(1)
 
@@ -274,7 +346,9 @@
         hidden[:, at] = hid
         h_t[at, :] = hid.T
 
+    weight_z(2, 0)
     exchange_wait(1, send_c, recv_c)
+    weight_z(2, 1)
 
     @pl.loop(0, d_tiles)
     def _(j):
@@ -282,9 +356,8 @@
         dw_down[:, at] = dot(h_t[...], recv_c[:, at], 1, 0).astype(BF)
 
     grad_r_start(2)
-    weight_z(2)
     grad_sum(2)
-    y_grad(2).start()
+    y_grad_start(2)
     weight_y(2)
     weight_r(2)
 
@@ -302,7 +375,7 @@
         at = tile_at(j, TILE)
         send_out[:, at] = dot(hidden[...], w_down[:, at], 1, 0).astype(BF)
 
-    exchange_start(2, send_out, ret_out, False)
+    back_start(2, send_out, ret_out, 1)
 
     @pl.loop(0, n_tiles)
     def _(j):
@@ -312,7 +385,7 @@
     grad_r_start(0)
     grad_z_start(2)
     grad_sum(0)
-    y_grad(0).start()
+    y_grad_start(0)
 
     @pl.loop(0, n_tiles)
     def _(j):
@@ -326,51 +399,92 @@
         at = tile_at(j, TILE)
         send_grad[:, at] = (dot(grad_a[...], w_gate[at, :], 1, 1) + dot(grad_b[...], w_up[at, :], 1, 1)).astype(BF)
 
-    exchange_start(3, send_grad, ret_grad, False)
+    back_start(3, send_grad, ret_grad, 1)
+    back_start(2, send_out, ret_out, 0)
+    back_start(3, send_grad, ret_grad, 0)
     grad_sum(1)
-    y_grad(0).wait_send()
-    y_grad(1).start()
+    y_grad_start(1)
     grad_z_start(0)
-
-    y_grad(1).wait_send()
-    exchange_start(2, send_out, ret_out, True)
-    exchange_start(3, send_grad, ret_grad, True)
+    back_wait(2, send_out, ret_out, 1)
+
+    @pl.loop(0, d_tiles)
+    def _(j):
+        at = tile_at(j, TILE)
+        rows_far = ret_out[half:, at]
+        far_send[0, :, at] = (
+            gates_far[:, 0:1] * dot(far[0], rows_far, 1, 0)
+            + gates_far[:, 1:2] * dot(far[1], rows_far, 1, 0)
+        ).astype(BF)
+
+    far_copy(0).start()
     grad_z_start(1)
-    exchange_wait(2, send_out, ret_out)
-
-    @pl.loop(0, d_tiles)
-    def _(j):
-        at = tile_at(j, TILE)
-        layer_out[:, at] = (
-            gates[:, 0:1] * dot(pick[0], ret_out[:, at], 1, 0)
-            + gates[:, 1:2] * dot(pick[1], ret_out[:, at], 1, 0)
-        ).astype(BF)
+    back_wait(3, send_grad, ret_grad, 1)
+
+    @pl.loop(0, d_tiles)
+    def _(j):
+        at = tile_at(j, TILE)
+        far_send[1, :, at] = dot(far[0] + far[1], ret_grad[half:, at], 1, 0).astype(BF)
+
+    far_copy(1).start()
+    back_wait(2, send_out, ret_out, 0)
+
+    @pl.loop(0, d_tiles)
+    def _(j):
+        at = tile_at(j, TILE)
+        rows_near = ret_out[:half, at]
+        pre_gate[:tok, at] = (
+            gates[:, 0:1] * dot(near[0], rows_near, 1, 0)
+            + gates[:, 1:2] * dot(near[1], rows_near, 1, 0)
+        )
+
+    back_wait(3, send_grad, ret_grad, 0)
+
+    @pl.loop(0, d_tiles)
+    def _(j):
+        at = tile_at(j, TILE)
+        pre_up[:tok, at] = dot(near[0] + near[1], ret_grad[:half, at], 1, 0)
 
     grad_end(2, out_down)
-    exchange_wait(3, send_grad, ret_grad)
-
-    @pl.loop(0, d_tiles)
-    def _(j):
-        at = tile_at(j, TILE)
-        grad_tokens[:, at] = dot(pick[0] + pick[1], ret_grad[:, at], 1, 0).astype(BF)
+    far_copy(0).wait_recv()
+
+    @pl.loop(0, tok // 64)
+    def _(i):
+        at = tile_at(i, 64)
+        layer_out[at, :] = (pre_gate[at, :] + far_recv[0, at, :].astype(F32)).astype(BF)
 
     grad_end(0, out_gate)
+    far_copy(1).wait_recv()
+
+    @pl.loop(0, tok // 64)
+    def _(i):
+        at = tile_at(i, 64)
+        grad_tokens[at, :] = (pre_up[at, :] + far_recv[1, at, :].astype(F32)).astype(BF)
+
     grad_end(1, out_up)
 
-    y_grad(2).wait_send()
     for w in range(3):
-        z_weight(w, relay.at[w]).wait_send()
-        y_weight(w, ins[w], b).wait_send()
-        z_grad(w).wait_send()
+        y_grad_sent(w)
+    for w in range(3):
+        for i in range(PIECES):
+            z_weight(w, i, relay.at[w, piece(i)]).wait_send()
+            y_weight(w, i, ins[w].at[piece(i)], b).wait_send()
+            z_grad(w, i).wait_send()
+            for p in range(1, nr):
+                for group in range(2):
+                    r_weight(w, i, group, ins[w].at[piece(i)], b, p, r).wait_send()
         for p in range(1, nr):
-            for group in range(2):
-                r_weight(w, group, ins[w], b, p, r).wait_send()
-                r_grad(w, p, group).wait_send()
-    for k, (src, dst) in enumerate(
-        ((send_x, recv_x), (send_c, recv_c), (send_out, ret_out), (send_grad, ret_grad))
-    ):
+            for side in range(2):
+                r_grad(w, p, side).wait_send()
+    for i in range(2):
+        info(i).wait_send()
+        far_copy(i).wait_send()
+    for k, (src, dst) in enumerate(((send_x, recv_x), (send_c, recv_c))):
         for p in range(1, experts):
             exchange(k, src, dst, p, me).wait_send()
+    for k, (src, dst) in ((2, (send_out, ret_out)), (3, (send_grad, ret_grad))):
+        for t in range(2):
+            for dl in range(1, nl):
+                back(k, src, dst, t, dl, l).wait_send()
 
 
 def store(*refs):
@@ -420,12 +534,15 @@
             pltpu.VMEM((3, rows, n_f), BF),
             pltpu.VMEM((3, rows, n_f), BF),
             slot_rows, slot_rows, slot_rows, slot_rows,
-            pltpu.VMEM((tok, 2), F32),
-            dma((6,)), dma((6,)), dma((6,)), dma((6,)),
-            dma((3, 2, nr - 1)), dma((3, 2, nr - 1)),
+            pltpu.VMEM((tok, 2), F32), pltpu.VMEM((tok, 2), F32),
+            pltpu.VMEM((2, tok, slots // 2), BF), pltpu.VMEM((2, tok, slots // 2), BF),
+            pltpu.VMEM((2, tok), jnp.int32), pltpu.VMEM((2, tok), F32),
+            pltpu.VMEM((2, tok, width), BF), pltpu.VMEM((2, tok, width), BF),
+            dma((6, PIECES)), dma((6, PIECES)), dma((6, PIECES)), dma((6, PIECES)),
+            dma((3, PIECES, 2, nr - 1)), dma((3, PIECES, 2, nr - 1)),
             dma((3, nr - 1, 2)), dma((3, nr - 1, 2)),
             dma((4, 2 * nl - 1)), dma((4, 2 * nl - 1)),
-            dma((3,)),
+            dma((3,)), dma((2,)), dma((2,)), dma((2,)), dma((2,)),
         ],
         compiler_params=pltpu.CompilerParams(
             collective_id=0, has_side_effects=True, vmem_limit_bytes=67043328

time: 183 us -> 173 us (0.945)
  the two profiles are of different devices: /device:TPU:6 before, /device:TPU:0 now
where the time goes in v2:
time: 173 us
  Pallas kernels  172 us (99%)
    pallas_call x1, Pallas kernels, shards(): step(swap_flags, tokens, route_ids.T, gate_values.T, out_grad, w_gate[0],...  168 us
    pallas_call x1, Pallas kernels, shards(): pl.pallas_call(store, out_shape=tuple((jax.ShapeDtypeStruct(out.shape, ou...  4.23 us

profile of v2, /device:TPU:0, one launch (start us, length us, event | category | flops | bytes accessed | tf_op | source)
XLA Modules:
  0.0 172.8 jit_solution(9982922411153297626)
XLA Ops:
  0.6 167.9 %shard_map.119 = (bf16[256,1024]{1,0:T(8,128)(2,1)}, bf16[256,1024]{1,0:T(8,128)(2,1)}, f32[256,1024]{1,0:T(8,128)}, f32[256,1024]{1,0:T(8,128)}, f32[256,1024]{1,0:T(8,128)}) custom-call(s32[8]{0:T(128)} %flags.1, bf16[256,1024]{1,0:T(8,128)(2,1)} %tokens.1, s32[2,256]{1,0:T(2,128)} %bitcast.11, f32[2,256]{1,0:T(2,128)} %bitcast.12, ...), custom_call_target="tpu_custom_call" | custom-call | tf_op jit(solution)/shard_map/pallas_call | solution.py:551
  168.5 4.2 %shard_map.120 = (bf16[256,1024]{1,0:T(8,128)(2,1)}, bf16[256,1024]{1,0:T(8,128)(2,1)}, f32[256,1024]{1,0:T(8,128)}, f32[256,1024]{1,0:T(8,128)}, f32[256,1024]{1,0:T(8,128)}) custom-call(bf16[256,1024]{1,0:T(8,128)(2,1)} %get-tuple-element.15.refs_0_, bf16[256,1024]{1,0:T(8,128)(2,1)} %get-tuple-element.16.refs_1_, f32[256,1024]{1,0:T(8,128)} %get-tuple-element.17.refs_2_, ...), custom_call_target="tpu_custom_call" | custom-call | tf_op jit(solution)/shard_map/pallas_call | solution.py:552

commit v3 on v2

--- a/solution.py
+++ b/solution.py
@@ -12,6 +12,7 @@
 MESH = pl.DeviceIdType.MESH
 TILE = 256
 PIECES = 2
+SPLIT = 4
 
 
 def dot(a, b, a_dim, b_dim):
@@ -23,13 +24,19 @@
 
 
 def kernel(
-    nl, nr, cap, flags, tokens, route_t, gates_t, out_grad, in_gate, in_up, in_down,
+    nl, nr, cap, flags, tokens_hbm, route_t, gates_t, out_grad_hbm, in_gate, in_up, in_down,
     layer_out, grad_tokens, out_gate, out_up, out_down,
-    pick, send_x, send_c, recv_x, recv_c, x_t, h_t, w_gate, w_up, w_down, relay,
+    tokens, out_grad, io_sem, pick, send_x, send_c, recv_x, recv_c, x_t, h_t, w_gate, w_up, w_down, relay,
     pre_gate, pre_up, hidden, grad_a, grad_b, dw_down, dw_gate, dw_up, from_r, from_y, to_z, from_z,
     send_out, send_grad, ret_out, ret_grad, gates, gates_far, near, far, route_p, gates_p, far_send, far_recv,
     z_s, z_r, y_s, y_r, w_s, w_r, g_s, g_r, d_s, d_r, own_sem, p_s, p_r, f_s, f_r,
 ):
+    def io(src, dst, i):
+        return pltpu.make_async_copy(src, dst, io_sem.at[i])
+
+    read_tokens, read_cot = io(tokens_hbm, tokens, 0), io(out_grad_hbm, out_grad, 1)
+    read_tokens.start()
+    read_cot.start()
     h, l, b, r = (lax.axis_index(name) for name in ("h", "l", "b", "r"))
     experts = 2 * nl
     rows, n_f = in_gate.shape
@@ -233,8 +240,8 @@
         at = pl.ds(pl.multiple_of((b * nr + r) * rows + i * chunk, chunk), chunk)
         return parts[w][at, :].astype(F32), from_y[w, tile_at(i, chunk), :].astype(F32)
 
-    def grad_z_start(w):
-        for k in range(PIECES):
+    def grad_z_start(w, which):
+        for k in which:
             y_grad(w, k).wait_recv()
 
             @pl.loop(k * piece_rows // chunk, (k + 1) * piece_rows // chunk)
@@ -288,6 +295,7 @@
     n_tiles = n_f // TILE
     d_tiles = tokens.shape[1] // TILE
     chosen = both.astype(F32).T.astype(BF)
+    read_tokens.wait()
 
     @pl.loop(0, d_tiles)
     def _(j):
@@ -296,6 +304,8 @@
     exchange_start(0, send_x, recv_x, False)
     exchange_start(0, send_x, recv_x, True)
     weight_start(1)
+    weight_start(2)
+    read_cot.wait()
     one_t, two_t = pick[0].astype(F32).T.astype(BF), pick[1].astype(F32).T.astype(BF)
 
     @pl.loop(0, d_tiles)
@@ -309,7 +319,6 @@
     weight_z(0, 0)
     weight_z(0, 1)
     exchange_start(1, send_c, recv_c, True)
-    weight_start(2)
     weight_y(0)
     weight_r(0)
     exchange_wait(0, send_x, recv_x)
@@ -347,8 +356,17 @@
         h_t[at, :] = hid.T
 
     weight_z(2, 0)
+    weight_z(2, 1)
+    weight_y(2)
+    weight_r(2)
+
+    @pl.loop(0, d_tiles)
+    def _(j):
+        at = tile_at(j, TILE)
+        send_out[:, at] = dot(hidden[...], w_down[:, at], 1, 0).astype(BF)
+
+    back_start(2, send_out, ret_out, 1)
     exchange_wait(1, send_c, recv_c)
-    weight_z(2, 1)
 
     @pl.loop(0, d_tiles)
     def _(j):
@@ -358,8 +376,6 @@
     grad_r_start(2)
     grad_sum(2)
     y_grad_start(2)
-    weight_y(2)
-    weight_r(2)
 
     @pl.loop(0, n_tiles)
     def _(j):
@@ -370,12 +386,6 @@
         grad_a[:, at] = (grad_h * up * sig * (1.0 + gate * (1.0 - sig))).astype(BF)
         grad_b[:, at] = (grad_h * gate * sig).astype(BF)
 
-    @pl.loop(0, d_tiles)
-    def _(j):
-        at = tile_at(j, TILE)
-        send_out[:, at] = dot(hidden[...], w_down[:, at], 1, 0).astype(BF)
-
-    back_start(2, send_out, ret_out, 1)
 
     @pl.loop(0, n_tiles)
     def _(j):
@@ -383,7 +393,7 @@
         dw_gate[:, at] = dot(x_t[...], grad_a[:, at], 1, 0).astype(BF)
 
     grad_r_start(0)
-    grad_z_start(2)
+    grad_z_start(2, (0, 1))
     grad_sum(0)
     y_grad_start(0)
 
@@ -404,7 +414,7 @@
     back_start(3, send_grad, ret_grad, 0)
     grad_sum(1)
     y_grad_start(1)
-    grad_z_start(0)
+    grad_z_start(0, (0, 1))
     back_wait(2, send_out, ret_out, 1)
 
     @pl.loop(0, d_tiles)
@@ -417,7 +427,7 @@
         ).astype(BF)
 
     far_copy(0).start()
-    grad_z_start(1)
+    grad_z_start(1, (0, 1))
     back_wait(3, send_grad, ret_grad, 1)
 
     @pl.loop(0, d_tiles)
@@ -488,8 +498,13 @@
 
 
 def store(*refs):
-    sems = refs[-1]
-    copies = [pltpu.make_async_copy(refs[i], refs[5 + i], sems.at[i]) for i in range(5)]
+    sources, targets, sems = refs[:5], refs[5:10], refs[10]
+    copies = []
+    for i in range(5):
+        size = sources[i].shape[0] // SPLIT
+        for k in range(SPLIT):
+            at = pl.ds(k * size, size)
+            copies.append(pltpu.make_async_copy(sources[i].at[at], targets[i].at[at], sems.at[i, k]))
     for copy in copies:
         copy.start()
     for copy in copies:
@@ -512,15 +527,17 @@
     step = pl.pallas_call(
         functools.partial(kernel, nl, nr, cap),
         out_shape=(
-            jax.ShapeDtypeStruct((tok, width), BF),
-            jax.ShapeDtypeStruct((tok, width), BF),
-            jax.ShapeDtypeStruct((rows, n_f), F32),
-            jax.ShapeDtypeStruct((rows, n_f), F32),
-            jax.ShapeDtypeStruct((rows, n_f), F32),
+            pltpu.VMEM((tok, width), BF),
+            pltpu.VMEM((tok, width), BF),
+            pltpu.VMEM((rows, n_f), F32),
+            pltpu.VMEM((rows, n_f), F32),
+            pltpu.VMEM((rows, n_f), F32),
         ),
-        in_specs=[pl.BlockSpec(memory_space=pltpu.SMEM), vmem, vmem, vmem, vmem, hbm, hbm, hbm],
+        in_specs=[pl.BlockSpec(memory_space=pltpu.SMEM), hbm, vmem, vmem, hbm, hbm, hbm, hbm],
         out_specs=(vmem,) * 5,
         scratch_shapes=[
+            pltpu.VMEM((tok, width), BF), pltpu.VMEM((tok, width), BF),
+            dma((2,)),
             pltpu.VMEM((2, tok, slots), BF),
             slot_rows, slot_rows, slot_rows, slot_rows,
             pltpu.VMEM((width, slots), BF), pltpu.VMEM((n_f, slots), BF),
@@ -545,7 +562,7 @@
             dma((3,)), dma((2,)), dma((2,)), dma((2,)), dma((2,)),
         ],
         compiler_params=pltpu.CompilerParams(
-            collective_id=0, has_side_effects=True, vmem_limit_bytes=67043328
+            collective_id=0, has_side_effects=True, vmem_limit_bytes=58 * 2**20
         ),
     )
     outs = step(swap_flags, tokens, route_ids.T, gate_values.T, out_grad, w_gate[0], w_up[0], w_down[0])
@@ -554,8 +571,9 @@
         out_shape=tuple(jax.ShapeDtypeStruct(out.shape, out.dtype) for out in outs),
         in_specs=[vmem] * 5,
         out_specs=(hbm,) * 5,
-        scratch_shapes=[dma((5,))],
-    )(*outs)
+        scratch_shapes=[dma((5, SPLIT))],
+        compiler_params=pltpu.CompilerParams(vmem_limit_bytes=2**20),
+    )(*(pltpu.with_memory_space_constraint(out, pltpu.VMEM) for out in outs))
     return outs[0], outs[1], outs[2][None], outs[3][None], outs[4][None]
 
 

time: 173 us -> 167 us (0.965)
  Pallas kernels: 172 us -> 164 us
    pallas_call x1, Pallas kernels: 168 us -> 162 us  [shards(): step(swap_flags, tokens, route_ids.T, gate_values.T, out_grad, w_gate[0],...]
    pallas_call x1, Pallas kernels: 4.23 us -> 2.17 us  [shards(): pl.pallas_call(store, out_shape=tuple((jax.ShapeDtypeStruct(out.shape, ou...]
where the time goes in v3:
time: 167 us; the launch traced here: 165 us
  Pallas kernels  164 us (98%)
    pallas_call x1, Pallas kernels, shards(): step(swap_flags, tokens, route_ids.T, gate_values.T, out_grad, w_gate[0],...  162 us

profile of v3, /device:TPU:0, one launch (start us, length us, event | category | flops | bytes accessed | tf_op | source)
XLA Modules:
  0.0 165.0 jit_solution(12175415999540903391)
XLA Ops:
  0.6 162.2 %shard_map.119 = (bf16[256,1024]{1,0:T(8,128)(2,1)S(1)}, bf16[256,1024]{1,0:T(8,128)(2,1)S(1)}, f32[256,1024]{1,0:T(8,128)S(1)}, f32[256,1024]{1,0:T(8,128)S(1)}, f32[256,1024]{1,0:T(8,128)S(1)}) custom-call(s32[8]{0:T(128)} %flags.1, bf16[256,1024]{1,0:T(8,128)(2,1)} %tokens_hbm.1, s32[2,256]{1,0:T(2,128)} %bitcast.11, f32[2,256]{1,0:T(2,128)} %bitcast.12, ...), custom_call_target="tpu_custom_call" | custom-call | tf_op jit(solution)/shard_map/pallas_call | solution.py:568
  162.9 2.2 %shard_map.120 = (bf16[256,1024]{1,0:T(8,128)(2,1)}, bf16[256,1024]{1,0:T(8,128)(2,1)}, f32[256,1024]{1,0:T(8,128)}, f32[256,1024]{1,0:T(8,128)}, f32[256,1024]{1,0:T(8,128)}) custom-call(bf16[256,1024]{1,0:T(8,128)(2,1)S(1)} %get-tuple-element.15.refs_0_, bf16[256,1024]{1,0:T(8,128)(2,1)S(1)} %get-tuple-element.16.refs_1_, ...), custom_call_target="tpu_custom_call" | custom-call | tf_op jit(solution)/shard_map/pallas_call | solution.py:569
